TPU v7x, 512 devices: a whole 4x4x16 slice. The times are simulated.
512 devices in a mesh: seq: 32 (over z_hi, x, core), sub: 16 (over z_lo, y).
Axes of the slice: x: 4, y: 4, z: 16 (z_hi: 4, z_lo: 4; z = z_hi * 4 + z_lo), core: 2. Of those that a mesh axis runs over, the one named last changes fastest.
Arguments:
- activations: bfloat16 [65536, 1024], P(('seq', 'sub')), may hold values from -6 to 6
- conv_weight: bfloat16 [5, 1152, 1024], P(None, 'sub'), may hold values from -1 to 1
- cotangent: bfloat16 [16384, 1152], P('seq', 'sub'), may hold values from -6 to 6
Outputs:
- features: bfloat16 [16384, 1152], P('seq', 'sub')
- input_grad: bfloat16 [65536, 1024], P(('seq', 'sub'))
- weight_grad: float32 [1024, 5, 1152], P('seq', None, 'sub')
All inputs are finite; a program needn't handle non-finite values.
Results may differ from a plain program's by a relative error of at most 0.02.
Values may be sent and summed in bfloat16 or wider, within the bound.
No kernel may reach another device: no remote copies, remote signals or barrier semaphores. Data moves between devices by JAX's collectives and lax.ppermute only.
A program may use at most 64 MiB of HBM per device.

v0:
```python
import jax
import jax.numpy as jnp
from jax import lax
from jax.sharding import PartitionSpec as P

EPSILON = 1e-06


def padded_2(block, sides, width):
    for axis, dim in sides:
        count = lax.axis_size(axis)
        forward = [(i, i + 1) for i in range(count - 1)]
        backward = [(target, source) for source, target in forward]
        low = lax.ppermute(
            lax.slice_in_dim(block, block.shape[dim] - width, None, axis=dim), axis, forward
        )
        high = lax.ppermute(lax.slice_in_dim(block, 0, width, axis=dim), axis, backward)
        block = jnp.concatenate([low, block, high], axis=dim)
    return block


def gelu_slope(tensor):
    return (
        0.5 * (1.0 + jax.scipy.special.erf(tensor * 0.7071067811865476))
        + tensor * jnp.exp(-0.5 * tensor * tensor) * 0.3989422804014327
    )


def pool_pairs(tensor):
    half_rows = tensor.shape[0] // 2
    return 0.5 * jnp.sum(tensor.reshape(half_rows, 2, tensor.shape[1]), axis=1)


def per_device(activations, conv_weight, cotangent):
    tap_count = conv_weight.shape[0]
    in_width = activations.shape[1]
    out_width = conv_weight.shape[1]
    full_out = out_width * lax.axis_size("sub")
    x_float = activations.astype(jnp.float32)
    inv_first = lax.rsqrt(jnp.mean(x_float * x_float, axis=1, keepdims=True) + EPSILON)
    normed_first = x_float * inv_first
    pooled = pool_pairs(jax.nn.gelu(normed_first, approximate=False)).astype(jnp.bfloat16)
    gathered = lax.all_gather(pooled, "sub", axis=0, tiled=True)
    block_rows = gathered.shape[0]
    padded = padded_2(gathered, (("seq", 0),), 2)
    conv_acc = jnp.zeros((block_rows, out_width), jnp.float32)
    for offset in range(tap_count):
        conv_acc = conv_acc + lax.dot_general(
            padded[offset : offset + block_rows],
            conv_weight[offset],
            (((1,), (1,)), ((), ())),
            preferred_element_type=jnp.float32,
        )
    conv_out = conv_acc.astype(jnp.bfloat16)
    y_float = conv_out.astype(jnp.float32)
    square_sum = lax.psum(jnp.sum(y_float * y_float, axis=1), "sub")
    inv_second = lax.rsqrt(square_sum / full_out + EPSILON)[:, None]
    normed_second = y_float * inv_second
    features = pool_pairs(jax.nn.gelu(normed_second, approximate=False)).astype(jnp.bfloat16)
    upstream = 0.5 * jnp.repeat(cotangent.astype(jnp.float32), 2, axis=0)
    slope_second = upstream * gelu_slope(normed_second)
    inner_second = lax.psum(jnp.sum(slope_second * normed_second, axis=1), "sub")
    conv_grad = (
        inv_second * (slope_second - normed_second * (inner_second / full_out)[:, None])
    ).astype(jnp.bfloat16)
    grad_padded = padded_2(conv_grad, (("seq", 0),), 2)
    running = jnp.zeros((block_rows, in_width), jnp.float32)
    for offset in range(tap_count):
        window = lax.dynamic_slice_in_dim(grad_padded, 0 + 4 - offset, block_rows, 0)
        running = running + jnp.dot(window, conv_weight[offset], preferred_element_type=jnp.float32)
    owned = lax.psum_scatter(
        running.astype(jnp.bfloat16), "sub", scatter_dimension=1, tiled=True
    ).astype(jnp.float32)
    pooled_grad = lax.all_to_all(
        owned.astype(jnp.bfloat16), "sub", split_axis=0, concat_axis=1, tiled=True
    ).astype(owned.dtype)
    slope_first = 0.5 * jnp.repeat(pooled_grad, 2, axis=0) * gelu_slope(normed_first)
    inner_first = jnp.mean(slope_first * normed_first, axis=1, keepdims=True)
    input_grad = (inv_first * (slope_first - normed_first * inner_first)).astype(jnp.bfloat16)
    pieces = [
        lax.dot_general(
            padded[offset : offset + block_rows],
            conv_grad,
            (((0,), (0,)), ((), ())),
            preferred_element_type=jnp.float32,
        )
        for offset in range(tap_count)
    ]
    weight_grad = lax.psum_scatter(
        jnp.stack(pieces, axis=1).astype(jnp.bfloat16), "seq", scatter_dimension=0, tiled=True
    ).astype(jnp.float32)
    return (features, input_grad, weight_grad)


def solution(mesh):
    return jax.shard_map(
        per_device,
        mesh=mesh,
        in_specs=(P(("seq", "sub"), None), P(None, "sub", None), P("seq", "sub")),
        out_specs=(P("seq", "sub"), P(("seq", "sub"), None), P("seq", None, "sub")),
        check_vma=False,
    )
```

profile of v0, /device:TPU:8, one launch (start us, length us, event | category | flops | bytes accessed | tf_op | source)
XLA Modules:
  0.0 446.3 jit_solution(8332122157335202841)
XLA Ops:
  7.2 1.1 fusion.93
  8.3 2.2 fusion.55
  12.7 91.6 %all-gather.2.cloned.1.call-done = bf16[1024,1024]{1,0:T(8,128)(2,1)} async-done(((bf16[64,1024]{1,0:T(8,128)(2,1)}), bf16[1024,1024]{1,0:T(8,128)(2,1)}) %all-gather.2.cloned.1.call-update) | async-done | bytes 2097168 | tf_op jit(solution)/shard_map/all_gather | solution.py:43
  104.3 0.9 fusion.151
  105.2 1.3 collective-permute-start
  106.5 1.3 collective-permute-start.1
  107.8 2.4 fusion.125
  110.3 0.9 collective-permute-done.1
  111.3 0.8 fusion.3
  112.1 0.7 fusion.9
  112.8 0.8 fusion.17
  113.6 1.7 multiply_reduce_fusion.1
  115.3 38.7 %psum.14 = f32[1024]{0:T(1024)S(1)} all-reduce(f32[1024]{0:T(1024)S(1)} %get-tuple-element.22), channel_id=1, replica_groups=mesh['seq'=32,'sub'=16] {'sub'}, use_global_device_ids=true, to_apply=%region_3.0 | all-reduce | flops 1024 | bytes 8192 | tf_op jit(solution)/shard_map/psum | solution.py:56
  154.2 42.8 %psum.15 = f32[1024]{0:T(1024)S(1)} all-reduce(f32[1024]{0:T(1024)S(1)} %get-tuple-element.14), channel_id=1, replica_groups=mesh['seq'=32,'sub'=16] {'sub'}, use_global_device_ids=true, to_apply=%region_6.0 | all-reduce | flops 1024 | bytes 8192 | tf_op jit(solution)/shard_map/psum | solution.py:62
  197.0 0.7 multiply_convert_fusion
  197.8 1.4 collective-permute-start.2
  199.2 1.7 fusion.123
  200.8 3.0 collective-permute-start.3
  203.9 0.8 fusion.117
  204.7 0.8 fusion.113
  205.5 0.8 fusion.110
  206.3 2.8 add_convert_fusion
  211.2 1.1 copy-done.3
  213.6 2.5 copy.17
  216.2 92.8 %reduce-scatter.3.cloned.1.call-done = bf16[1024,64]{0,1:T(8,128)(2,1)} async-done(((bf16[1024,1024]{0,1:T(8,128)(2,1)}), bf16[1024,64]{0,1:T(8,128)(2,1)}) %reduce-scatter.3.cloned.1.call-update) | async-done | bytes 131088 | tf_op jit(solution)/shard_map/reduce_scatter | solution.py:71
  308.9 1.1 copy.20
  310.0 0.9 reshape.40
  310.9 8.1 %all-to-all-start = ((bf16[16,2,2048]{2,1,0:T(2,128)(2,1)}), bf16[16,2,2048]{2,1,0:T(2,128)(2,1)S(1)}, u32[]{:S(2)}, u32[]{:S(2)}) async-start(bf16[16,2,2048]{2,1,0:T(2,128)(2,1)} %reshape.40), calls=%async_computation.1 | async-start | bytes 262144 | tf_op jit(solution)/shard_map/all_to_all | solution.py:74
  319.9 0.7 copy.18
  320.6 114.9 %reduce-scatter.5.cloned.1.call-done = bf16[32,5,72]{2,1,0:T(8,128)(2,1)} async-done(((bf16[1024,5,72]{2,1,0:T(8,128)(2,1)}), bf16[32,5,72]{2,1,0:T(8,128)(2,1)}) %reduce-scatter.5.cloned.1.call-update) | async-done | bytes 23056 | tf_op jit(solution)/shard_map/reduce_scatter | solution.py:89
  435.5 1.5 copy.19
  438.8 1.0 fusion.90
  (53 shorter events, 8.7 us)
Async XLA Ops:
  7.2 5.0 %copy-start.6 = (bf16[512,72]{0,1:T(8,128)(2,1)S(1)}, bf16[512,72]{0,1:T(8,128)(2,1)}, u32[]{:S(2)}) copy-start(bf16[512,72]{0,1:T(8,128)(2,1)} %param.5) | copy-start | bytes 221188
  7.2 97.1 %all-gather.2.cloned.1.call-start = ((), (), s32[]{:S(2)}) async-start(), calls=%async_computation.3 | async-start | bytes 2228224 | tf_op jit(solution)/shard_map/all_gather | solution.py:43
  10.5 97.3 %copy-start.4 = (bf16[5,72,1024]{2,1,0:T(8,128)(2,1)S(1)}, bf16[5,72,1024]{2,1,0:T(8,128)(2,1)}, u32[]{:S(2)}) copy-start(bf16[5,72,1024]{2,1,0:T(8,128)(2,1)} %param.4) | copy-start | bytes 2211844
  12.1 296.8 %reduce-scatter.3.cloned.1.call-start = ((), (), s32[]{:S(2)}) async-start(), calls=%async_computation.4 | async-start | bytes 2228224 | tf_op jit(solution)/shard_map/reduce_scatter | solution.py:71
  104.3 5.9 %copy-start = (bf16[1024,1024]{1,0:T(8,128)(2,1)S(1)}, bf16[1024,1024]{1,0:T(8,128)(2,1)}, u32[]{:S(2)}) copy-start(bf16[1024,1024]{1,0:T(8,128)(2,1)} %all-gather.2.cloned.1.call-done) | copy-start | bytes 6291460
  105.2 6.8 %collective-permute-start = (bf16[2,1024]{1,0:T(2,128)(2,1)S(1)}, bf16[2,1024]{1,0:T(2,128)(2,1)S(1)}, u32[]{:S(2)}, u32[]{:S(2)}) collective-permute-start(bf16[2,1024]{1,0:T(2,128)(2,1)S(1)} %get-tuple-element.16), channel_id=1, source_target_pairs={{0,16},{16,32},{32,48},{48,64},{64,80},{80,96},{96,112},{112,128},... | collective-permute-start | bytes 12296 | tf_op jit(solution)/shard_map/ppermute | solution.py:14
  106.5 4.8 %collective-permute-start.1 = (bf16[2,1024]{1,0:T(2,128)(2,1)S(1)}, bf16[2,1024]{1,0:T(2,128)(2,1)S(1)}, u32[]{:S(2)}, u32[]{:S(2)}) collective-permute-start(bf16[2,1024]{1,0:T(2,128)(2,1)S(1)} %get-tuple-element.17), channel_id=1, source_target_pairs={{16,0},{32,16},{48,32},{64,48},{80,64},{96,80},{112,96},{128,112},... | collective-permute-start | bytes 12296 | tf_op jit(solution)/shard_map/ppermute | solution.py:17
  111.3 2.3 copy-start.2
  197.8 6.1 %copy-start.5 = (bf16[5,72,1024]{2,1,0:T(8,128)(2,1)S(1)}, bf16[5,72,1024]{2,1,0:T(8,128)(2,1)}, u32[]{:S(2)}) copy-start(bf16[5,72,1024]{2,1,0:T(8,128)(2,1)} %param.4) | copy-start | bytes 2211844
  197.8 6.1 %collective-permute-start.2 = (bf16[2,72]{0,1:T(8,128)(2,1)S(1)}, bf16[2,72]{0,1:T(8,128)(2,1)S(1)}, u32[]{:S(2)}, u32[]{:S(2)}) collective-permute-start(bf16[2,72]{0,1:T(8,128)(2,1)S(1)} %get-tuple-element.20), channel_id=1, source_target_pairs={{16,0},{32,16},{48,32},{64,48},{80,64},{96,80},{112,96},{128,112},... | collective-permute-start | bytes 872 | tf_op jit(solution)/shard_map/ppermute | solution.py:17
  200.8 4.7 %collective-permute-start.3 = (bf16[2,72]{0,1:T(8,128)(2,1)S(1)}, bf16[2,72]{0,1:T(8,128)(2,1)S(1)}, u32[]{:S(2)}, u32[]{:S(2)}) collective-permute-start(bf16[2,72]{0,1:T(8,128)(2,1)S(1)} %get-tuple-element.21), channel_id=1, source_target_pairs={{0,16},{16,32},{32,48},{48,64},{64,80},{80,96},{96,112},{112,128},... | collective-permute-start | bytes 872 | tf_op jit(solution)/shard_map/ppermute | solution.py:14
  209.1 226.4 %reduce-scatter.5.cloned.1.call-start = ((), (), s32[]{:S(2)}) async-start(), calls=%async_computation.5 | async-start | bytes 2162688 | tf_op jit(solution)/shard_map/reduce_scatter | solution.py:89
  210.7 1.6 copy-start.3
  310.9 126.1 %all-to-all-start = ((bf16[16,2,2048]{2,1,0:T(2,128)(2,1)}), bf16[16,2,2048]{2,1,0:T(2,128)(2,1)S(1)}, u32[]{:S(2)}, u32[]{:S(2)}) async-start(bf16[16,2,2048]{2,1,0:T(2,128)(2,1)} %reshape.40), calls=%async_computation.1 | async-start | bytes 262144 | tf_op jit(solution)/shard_map/all_to_all | solution.py:74
  437.2 1.1 copy-start.1
Sparse Core Ops, SparseCore 0:
  12.2 92.0 all-gather.1
  209.3 99.6 reduce-scatter.2
  313.3 122.1 reduce-scatter.4
where the time goes:
time: 447 us; the launch traced here: 446 us
  waiting for transfers between devices  300 us (67%)
  blocking collectives  81.5 us (18%)
  matrix products  16.3 us (4%)
  starting transfers between devices  15.5 us (3%)
  between operations  14 us (3%)
  local copies, waits for them, and re-layouts  11.2 us (3%)
  other arithmetic  7.52 us (2%)
    reduce_scatter x1, waiting for transfers between devices, per_device(): lax.psum_scatter(jnp.stack(pieces, axis=1).astype(jnp.bfloat16), 'seq', s...  115 us
    reduce_scatter x1, waiting for transfers between devices, per_device(): lax.psum_scatter(running.astype(jnp.bfloat16), 'sub', scatter_dimension=1...  92.8 us
    all_gather x1, waiting for transfers between devices, per_device(): gathered = lax.all_gather(pooled, 'sub', axis=0, tiled=True)  91.6 us
    psum x1, blocking collectives, per_device(): lax.psum(jnp.sum(slope_second * normed_second, axis=1), 'sub')  42.8 us
    psum x1, blocking collectives, per_device(): square_sum = lax.psum(jnp.sum(y_float * y_float, axis=1), 'sub')  38.7 us
  transfers between devices with their start and end apart: 8, of which 4 were waited for; matrix products, arithmetic and copies ran while one was open for 4% of the time, Pallas kernels for 0%

commit v1 on v0

--- a/solution.py
+++ b/solution.py
@@ -40,7 +40,9 @@
     inv_first = lax.rsqrt(jnp.mean(x_float * x_float, axis=1, keepdims=True) + EPSILON)
     normed_first = x_float * inv_first
     pooled = pool_pairs(jax.nn.gelu(normed_first, approximate=False)).astype(jnp.bfloat16)
-    gathered = lax.all_gather(pooled, "sub", axis=0, tiled=True)
+    gathered = jnp.concatenate(
+        lax.all_to_all(jnp.stack([pooled] * lax.axis_size("sub")), "sub", 0, 0), axis=0
+    )
     block_rows = gathered.shape[0]
     padded = padded_2(gathered, (("seq", 0),), 2)
     conv_acc = jnp.zeros((block_rows, out_width), jnp.float32)

time: 447 us -> 412 us (0.922)
  waiting for transfers between devices: 300 us -> 253 us
  starting transfers between devices: 15.5 us -> 24.8 us
  blocking collectives: 81.5 us -> 86.1 us
    all_gather x1 -> x0, waiting for transfers between devices: 91.6 us -> none  [per_device(): gathered = lax.all_gather(pooled, 'sub', axis=0, tiled=True)]
    all_to_all x0 -> x1, waiting for transfers between devices: none -> 40.4 us  [per_device(): lax.all_to_all(jnp.stack([pooled] * lax.axis_size('sub')), 'sub', 0, 0)]
    all_to_all x0 -> x1, starting transfers between devices: none -> 9.43 us  [per_device(): lax.all_to_all(jnp.stack([pooled] * lax.axis_size('sub')), 'sub', 0, 0)]
    psum x1, blocking collectives: 38.7 us -> 43.2 us  [per_device(): square_sum = lax.psum(jnp.sum(y_float * y_float, axis=1), 'sub')]
where the time goes in v1:
time: 412 us; the launch traced here: 411 us
  waiting for transfers between devices  253 us (61%)
  blocking collectives  86.1 us (21%)
  starting transfers between devices  24.8 us (6%)
  matrix products  15.7 us (4%)
  between operations  14.3 us (3%)
  local copies, waits for them, and re-layouts  10.6 us (3%)
  other arithmetic  6.85 us (2%)
    reduce_scatter x1, waiting for transfers between devices, per_device(): lax.psum_scatter(jnp.stack(pieces, axis=1).astype(jnp.bfloat16), 'seq', s...  115 us
    reduce_scatter x1, waiting for transfers between devices, per_device(): lax.psum_scatter(running.astype(jnp.bfloat16), 'sub', scatter_dimension=1...  95.8 us
    psum x1, blocking collectives, per_device(): square_sum = lax.psum(jnp.sum(y_float * y_float, axis=1), 'sub')  43.2 us
    psum x1, blocking collectives, per_device(): lax.psum(jnp.sum(slope_second * normed_second, axis=1), 'sub')  42.9 us
    all_to_all x1, waiting for transfers between devices, per_device(): lax.all_to_all(jnp.stack([pooled] * lax.axis_size('sub')), 'sub', 0, 0)  40.4 us
    all_to_all x1, starting transfers between devices, per_device(): lax.all_to_all(jnp.stack([pooled] * lax.axis_size('sub')), 'sub', 0, 0)  9.43 us
  transfers between devices with their start and end apart: 8, of which 4 were waited for; matrix products, arithmetic and copies ran while one was open for 4% of the time, Pallas kernels for 0%

profile of v1, /device:TPU:8, one launch (start us, length us, event | category | flops | bytes accessed | tf_op | source)
XLA Modules:
  0.0 411.4 jit_solution(12284457120379499315)
XLA Ops:
  7.2 1.1 fusion.66
  8.3 2.2 fusion.28
  11.4 1.6 stack.20
  13.0 9.4 %all-to-all-start = ((bf16[16,64,1024]{2,1,0:T(8,128)(2,1)}), bf16[16,64,1024]{2,1,0:T(8,128)(2,1)S(1)}, u32[]{:S(2)}, u32[]{:S(2)}) async-start(bf16[16,64,1024]{2,1,0:T(8,128)(2,1)} %stack.20), calls=%async_computation | async-start | bytes 4194304 | tf_op jit(solution)/shard_map/all_to_all | solution.py:44
  23.0 40.4 %all-to-all-done = bf16[16,64,1024]{2,1,0:T(8,128)(2,1)S(1)} async-done(((bf16[16,64,1024]{2,1,0:T(8,128)(2,1)}), bf16[16,64,1024]{2,1,0:T(8,128)(2,1)S(1)}, u32[]{:S(2)}, u32[]{:S(2)}) %all-to-all-start) | async-done | bytes 2097184 | tf_op jit(solution)/shard_map/all_to_all | solution.py:44
  63.4 1.3 collective-permute-start
  64.7 1.3 collective-permute-start.1
  66.0 1.7 fusion.98
  67.7 1.8 collective-permute-done.1
  69.5 0.8 fusion.4
  70.3 0.7 fusion.2
  71.0 0.8 fusion.7
  71.8 1.7 multiply_reduce_fusion.1
  73.5 43.2 %psum.14 = f32[1024]{0:T(1024)S(1)} all-reduce(f32[1024]{0:T(1024)S(1)} %get-tuple-element.22), channel_id=1, replica_groups=mesh['seq'=32,'sub'=16] {'sub'}, use_global_device_ids=true, to_apply=%region_3.0 | all-reduce | flops 1024 | bytes 8192 | tf_op jit(solution)/shard_map/psum | solution.py:58
  116.9 42.9 %psum.15 = f32[1024]{0:T(1024)S(1)} all-reduce(f32[1024]{0:T(1024)S(1)} %get-tuple-element.14), channel_id=1, replica_groups=mesh['seq'=32,'sub'=16] {'sub'}, use_global_device_ids=true, to_apply=%region_6.0 | all-reduce | flops 1024 | bytes 8192 | tf_op jit(solution)/shard_map/psum | solution.py:64
  159.8 0.7 multiply_convert_fusion
  160.6 1.4 collective-permute-start.2
  162.0 1.7 fusion.96
  163.6 3.0 collective-permute-start.3
  166.7 0.8 fusion.90
  167.5 0.8 fusion.86
  168.3 0.8 fusion.83
  169.1 2.8 add_convert_fusion
  175.4 2.5 copy.17
  177.9 95.8 %reduce-scatter.3.cloned.1.call-done = bf16[1024,64]{0,1:T(8,128)(2,1)} async-done(((bf16[1024,1024]{0,1:T(8,128)(2,1)}), bf16[1024,64]{0,1:T(8,128)(2,1)}) %reduce-scatter.3.cloned.1.call-update) | async-done | bytes 131088 | tf_op jit(solution)/shard_map/reduce_scatter | solution.py:73
  273.6 1.1 copy.20
  274.7 0.9 reshape.46
  275.6 8.1 %all-to-all-start.1 = ((bf16[16,2,2048]{2,1,0:T(2,128)(2,1)}), bf16[16,2,2048]{2,1,0:T(2,128)(2,1)S(1)}, u32[]{:S(2)}, u32[]{:S(2)}) async-start(bf16[16,2,2048]{2,1,0:T(2,128)(2,1)} %reshape.46), calls=%async_computation.2 | async-start | bytes 262144 | tf_op jit(solution)/shard_map/all_to_all | solution.py:76
  284.6 0.7 copy.18
  285.3 115.1 %reduce-scatter.5.cloned.1.call-done = bf16[32,5,72]{2,1,0:T(8,128)(2,1)} async-done(((bf16[1024,5,72]{2,1,0:T(8,128)(2,1)}), bf16[32,5,72]{2,1,0:T(8,128)(2,1)}) %reduce-scatter.5.cloned.1.call-update) | async-done | bytes 23056 | tf_op jit(solution)/shard_map/reduce_scatter | solution.py:91
  400.4 1.5 copy.19
  403.6 0.9 fusion.63
  (45 shorter events, 7.8 us)
Async XLA Ops:
  13.0 9.5 %copy-start.3 = (bf16[512,72]{0,1:T(8,128)(2,1)S(1)}, bf16[512,72]{0,1:T(8,128)(2,1)}, u32[]{:S(2)}) copy-start(bf16[512,72]{0,1:T(8,128)(2,1)} %param.5) | copy-start | bytes 221188
  13.0 50.4 %all-to-all-start = ((bf16[16,64,1024]{2,1,0:T(8,128)(2,1)}), bf16[16,64,1024]{2,1,0:T(8,128)(2,1)S(1)}, u32[]{:S(2)}, u32[]{:S(2)}) async-start(bf16[16,64,1024]{2,1,0:T(8,128)(2,1)} %stack.20), calls=%async_computation | async-start | bytes 4194304 | tf_op jit(solution)/shard_map/all_to_all | solution.py:44
  22.4 251.2 %reduce-scatter.3.cloned.1.call-start = ((), (), s32[]{:S(2)}) async-start(), calls=%async_computation.4 | async-start | bytes 2228224 | tf_op jit(solution)/shard_map/reduce_scatter | solution.py:73
  23.0 46.5 %copy-start.1 = (bf16[5,72,1024]{2,1,0:T(8,128)(2,1)S(1)}, bf16[5,72,1024]{2,1,0:T(8,128)(2,1)}, u32[]{:S(2)}) copy-start(bf16[5,72,1024]{2,1,0:T(8,128)(2,1)} %param.4) | copy-start | bytes 2211844
  63.4 6.9 %collective-permute-start = (bf16[2,1024]{1,0:T(2,128)(2,1)S(1)}, bf16[2,1024]{1,0:T(2,128)(2,1)S(1)}, u32[]{:S(2)}, u32[]{:S(2)}) collective-permute-start(bf16[2,1024]{1,0:T(2,128)(2,1)S(1)} %get-tuple-element.16), channel_id=1, source_target_pairs={{0,16},{16,32},{32,48},{48,64},{64,80},{80,96},{96,112},{112,128},... | collective-permute-start | bytes 12296 | tf_op jit(solution)/shard_map/ppermute | solution.py:14
  64.7 4.8 %collective-permute-start.1 = (bf16[2,1024]{1,0:T(2,128)(2,1)S(1)}, bf16[2,1024]{1,0:T(2,128)(2,1)S(1)}, u32[]{:S(2)}, u32[]{:S(2)}) collective-permute-start(bf16[2,1024]{1,0:T(2,128)(2,1)S(1)} %get-tuple-element.17), channel_id=1, source_target_pairs={{16,0},{32,16},{48,32},{64,48},{80,64},{96,80},{112,96},{128,112},... | collective-permute-start | bytes 12296 | tf_op jit(solution)/shard_map/ppermute | solution.py:17
  160.6 6.1 %copy-start.2 = (bf16[5,72,1024]{2,1,0:T(8,128)(2,1)S(1)}, bf16[5,72,1024]{2,1,0:T(8,128)(2,1)}, u32[]{:S(2)}) copy-start(bf16[5,72,1024]{2,1,0:T(8,128)(2,1)} %param.4) | copy-start | bytes 2211844
  160.6 6.1 %collective-permute-start.2 = (bf16[2,72]{0,1:T(8,128)(2,1)S(1)}, bf16[2,72]{0,1:T(8,128)(2,1)S(1)}, u32[]{:S(2)}, u32[]{:S(2)}) collective-permute-start(bf16[2,72]{0,1:T(8,128)(2,1)S(1)} %get-tuple-element.20), channel_id=1, source_target_pairs={{16,0},{32,16},{48,32},{64,48},{80,64},{96,80},{112,96},{128,112},... | collective-permute-start | bytes 872 | tf_op jit(solution)/shard_map/ppermute | solution.py:17
  163.6 4.7 %collective-permute-start.3 = (bf16[2,72]{0,1:T(8,128)(2,1)S(1)}, bf16[2,72]{0,1:T(8,128)(2,1)S(1)}, u32[]{:S(2)}, u32[]{:S(2)}) collective-permute-start(bf16[2,72]{0,1:T(8,128)(2,1)S(1)} %get-tuple-element.21), channel_id=1, source_target_pairs={{0,16},{16,32},{32,48},{48,64},{64,80},{80,96},{96,112},{112,128},... | collective-permute-start | bytes 872 | tf_op jit(solution)/shard_map/ppermute | solution.py:14
  171.9 228.5 %reduce-scatter.5.cloned.1.call-start = ((), (), s32[]{:S(2)}) async-start(), calls=%async_computation.5 | async-start | bytes 2162688 | tf_op jit(solution)/shard_map/reduce_scatter | solution.py:91
  275.6 126.3 %all-to-all-start.1 = ((bf16[16,2,2048]{2,1,0:T(2,128)(2,1)}), bf16[16,2,2048]{2,1,0:T(2,128)(2,1)S(1)}, u32[]{:S(2)}, u32[]{:S(2)}) async-start(bf16[16,2,2048]{2,1,0:T(2,128)(2,1)} %reshape.46), calls=%async_computation.2 | async-start | bytes 262144 | tf_op jit(solution)/shard_map/all_to_all | solution.py:76
  402.1 1.1 copy-start
Sparse Core Ops, SparseCore 0:
  172.1 101.5 reduce-scatter.2
  278.0 122.3 reduce-scatter.4
